TPU v7x, 256 devices: a whole 4x4x8 slice. The times are simulated.
256 devices in a mesh: seq: 64 (over z, y, core), dp: 4 (over x).
Axes of the slice: x: 4, y: 4, z: 8, core: 2. Of those that a mesh axis runs over, the one named last changes fastest.
Arguments:
- queries: bfloat16 [131072, 1024], P(('dp', 'seq')), parts along dimension 0, may hold values from -5 to 5
- key_input: bfloat16 [131072, 128], P(('dp', 'seq')), parts along dimension 0, may hold values from -5 to 5
- value_input: bfloat16 [131072, 128], P(('dp', 'seq')), parts along dimension 0, may hold values from -5 to 5
- attn_out: bfloat16 [131072, 1024], P(('dp', 'seq')), parts along dimension 0, may hold values from -3 to 3
- out_grad: bfloat16 [131072, 1024], P(('dp', 'seq')), parts along dimension 0, may hold values from -5 to 5
- log_norm: float32 [131072, 8], P(('dp', 'seq')), parts along dimension 0, may hold values from 4 to 6
- doc_block: int32 [1024], P('dp'), parts along dimension 0, may hold values from 0 to 127, as said below
Outputs:
- query_grad: bfloat16 [131072, 1024], P(('dp', 'seq')), parts along dimension 0
- key_grad: bfloat16 [131072, 128], P(('dp', 'seq')), parts along dimension 0
- value_grad: bfloat16 [131072, 128], P(('dp', 'seq')), parts along dimension 0
There are 4 independent parts, one for each index of `dp`. A program takes and returns all parts, laid end to end along the dimension named above; each array names one. Nothing has to cross between parts.
Inputs may be any that keep to these rules, and one draw needn't show every extreme that they name: `doc_block`: ids never fall along the sequence and rise by at most one from block to block; every id of 0 to 127 covers 1 to 8 consecutive blocks; id 0 covers exactly the first 8 blocks.
All inputs are finite; a program needn't handle non-finite values.
Results may differ from a plain program's by a relative error of at most 0.0052.
Values may be sent and summed in bfloat16 or wider, within the bound.
No kernel may reach another device: no remote copies, remote signals or barrier semaphores. Data moves between devices by JAX's collectives and lax.ppermute only.
A program may use at most 64 MiB of HBM per device.

v0:
```python
import functools

import jax
import jax.numpy as jnp
from jax import lax
from jax.experimental import pallas as pl
from jax.experimental.pallas import tpu as pltpu
from jax.sharding import PartitionSpec as P

BLK = 128
H = 8
DH = 128
TOK = 512
NB = TOK // BLK
HALF = TOK // 2
FAR_TOK = 3 * BLK
LOG2E = 1.4426950408889634
SCALE = DH**-0.5
FAR = -1e30
F32 = jnp.float32
BF16 = jnp.bfloat16
NT = (((1,), (1,)), ((), ()))
NN = (((1,), (0,)), ((), ()))
ANY = pl.BlockSpec(memory_space=pl.ANY)
SMEM = pl.BlockSpec(memory_space=pltpu.SMEM)
VMEM = pl.BlockSpec(memory_space=pltpu.VMEM)
VMEM_LIMIT = 40 << 20
EARLY_LIMIT = 56 << 20
HEADS_A = 4


def dot(a, b, dims):
    return lax.dot_general(a, b, dims, preferred_element_type=F32)


def device_index():
    return lax.axis_index("seq")


def own_starts(doc):
    first = device_index() * NB
    starts = [jnp.int32(0)]
    for i in range(1, NB):
        same = doc[first + i] == doc[first + i - 1]
        starts.append(jnp.where(same, starts[-1], jnp.int32(i)))
    return starts


def crossing(doc, distance):
    me = device_index()
    first = me * NB
    key_first = first - NB * distance
    valid = key_first >= 0
    near = jnp.maximum(key_first, 0)
    keys = jnp.int32(0)
    rows = jnp.int32(0)
    for j in range(NB):
        keys += jnp.where(doc[near + j] == doc[first], 1, 0)
        rows += jnp.where(doc[first + j] == doc[near + NB - 1], 1, 0)
    return jnp.where(valid, keys, 0), jnp.where(valid, rows, 0)


def cols(h):
    return pl.ds(pl.multiple_of(h * DH, DH), DH)


def row(h):
    return pl.ds(h, 1)


def piece(k, v, k_t, q, g, lnorm, delta, bias):
    s = dot(k, q, NT) * (SCALE * LOG2E) - lnorm
    if bias is not None:
        s = s + bias
    p = jnp.exp2(s)
    ds = (p * (dot(v, g, NT) - delta)).astype(BF16)
    dv = dot(p.astype(BF16), g, NN)
    dk = dot(ds, q, NN)
    dq_t = dot(k_t, ds, NN)
    return dq_t, dk, dv


def fill_bias(doc, bias):
    starts = own_starts(doc)
    key = lax.broadcasted_iota(jnp.int32, (TOK, BLK), 0)
    for i in range(NB):
        tok = lax.broadcasted_iota(jnp.int32, (TOK, BLK), 1) + i * BLK
        ok = (key <= tok) & (key >= starts[i] * BLK)
        bias[:, i * BLK : (i + 1) * BLK] = jnp.where(ok, 0.0, FAR).astype(F32)


def own_head(q, g, k, v, k_t, ln, delta, bias, dkv):
    low = slice(0, HALF)
    high = slice(HALF, TOK)
    x0, dk0, dv0 = piece(k[low, :], v[low, :], k_t[:, low], q, g, ln, delta, bias[low, :])
    x1, dk1, dv1 = piece(
        k[high, :], v[high, :], k_t[:, high], q[high, :], g[high, :], ln[:, high], delta[:, high], bias[high, high]
    )
    for rows, dk, dv in ((low, dk0, dv0), (high, dk1, dv1)):
        dkv[rows, 0:DH] += dk
        dkv[rows, DH:] += dv
    return x0[:, low], x0[:, high] + x1


def head_delta(g, a):
    prod = g.astype(F32) * a.astype(F32)
    top = prod.astype(BF16)
    rest = (prod - top.astype(F32)).astype(BF16)
    ones = jnp.ones((8, 2 * DH), BF16)
    return dot(ones, jnp.concatenate([top, rest], axis=1), NT)[0:1, :]


def early_kernel(
    doc, q_hbm, k_hbm, v_hbm, a_hbm, g_hbm, ln_hbm,
    delta_out, dqt_out, dkv_out, far_out,
    q, g, a, k, v, k_t, ln, delta, bias, dq_t, dkv, far, sem_q, sem_g, sem_a, sem_s, sem_o,
):
    small = [
        pltpu.make_async_copy(k_hbm, k, sem_s.at[0]),
        pltpu.make_async_copy(v_hbm, v, sem_s.at[1]),
        pltpu.make_async_copy(ln_hbm, ln, sem_s.at[2]),
    ]

    def copy_q(h):
        return pltpu.make_async_copy(q_hbm.at[:, cols(h)], q.at[h], sem_q.at[h])

    def copy_g(h):
        return pltpu.make_async_copy(g_hbm.at[:, cols(h)], g.at[h], sem_g.at[h])

    def copy_a(h):
        return pltpu.make_async_copy(a_hbm.at[:, cols(h)], a.at[h], sem_a.at[h])

    def copy_o(h):
        return pltpu.make_async_copy(dq_t.at[h], dqt_out.at[h], sem_o.at[h])

    for c in small:
        c.start()
    for h in range(H):
        copy_g(h).start()
        copy_a(h).start()
        if h < HEADS_A:
            copy_q(h).start()
    fill_bias(doc, bias)
    dkv[...] = jnp.zeros((TOK, 2 * DH), F32)
    for c in small:
        c.wait()
    k_t[...] = jnp.transpose(k[...])
    far[:, 0:DH] = k[BLK:, :]
    far[:, DH:] = v[BLK:, :]

    @pl.loop(0, H, unroll=2)
    def _(h):
        copy_g(h).wait()
        copy_a(h).wait()
        delta[row(h), :] = head_delta(g[h], a[h])

    @pl.loop(0, HEADS_A, unroll=2)
    def _(h):
        copy_q(h).wait()
        lo, hi = own_head(q[h], g[h], k, v, k_t, ln[row(h), :] * LOG2E, delta[row(h), :], bias, dkv)
        dq_t[h, :, 0:HALF] = lo
        dq_t[h, :, HALF:] = hi
        copy_o(h).start()

    tail = [
        pltpu.make_async_copy(delta, delta_out, sem_s.at[0]),
        pltpu.make_async_copy(dkv, dkv_out, sem_s.at[1]),
        pltpu.make_async_copy(far, far_out, sem_s.at[2]),
    ]
    for c in tail:
        c.start()
    for h in range(HEADS_A):
        copy_o(h).wait()
    for c in tail:
        c.wait()


def early(doc, q, k, v, a, g, ln_t):
    big = pltpu.VMEM((H, TOK, DH), BF16)
    return pl.pallas_call(
        early_kernel,
        name="early",
        out_shape=(
            jax.ShapeDtypeStruct((H, TOK), F32),
            jax.ShapeDtypeStruct((HEADS_A, DH, TOK), F32),
            jax.ShapeDtypeStruct((TOK, 2 * DH), F32),
            jax.ShapeDtypeStruct((FAR_TOK, 2 * DH), BF16),
        ),
        in_specs=[SMEM] + [ANY] * 6,
        out_specs=(ANY,) * 4,
        scratch_shapes=[
            big, big, big,
            pltpu.VMEM((TOK, DH), BF16),
            pltpu.VMEM((TOK, DH), BF16),
            pltpu.VMEM((DH, TOK), BF16),
            pltpu.VMEM((H, TOK), F32),
            pltpu.VMEM((H, TOK), F32),
            pltpu.VMEM((TOK, TOK), F32),
            pltpu.VMEM((HEADS_A, DH, TOK), F32),
            pltpu.VMEM((TOK, 2 * DH), F32),
            pltpu.VMEM((FAR_TOK, 2 * DH), BF16),
            pltpu.SemaphoreType.DMA((H,)),
            pltpu.SemaphoreType.DMA((H,)),
            pltpu.SemaphoreType.DMA((H,)),
            pltpu.SemaphoreType.DMA((3,)),
            pltpu.SemaphoreType.DMA((H,)),
        ],
        compiler_params=pltpu.CompilerParams(vmem_limit_bytes=EARLY_LIMIT),
        cost_estimate=pl.CostEstimate(flops=4_000_000_000, bytes_accessed=6_000_000, transcendentals=1_600_000),
    )(doc, q, k, v, a, g, ln_t)


def remote_kernel(distance, *refs):
    if distance == 1:
        doc, q, g, ln, delta, k_in, v_in, dqt_out, kvg_out = refs[:9]
        total = TOK
    else:
        doc, q, g, ln, delta, kv_in, dqt_out, kvg_out = refs[:8]
        total = FAR_TOK
    k, k_t, ln2, dq_t, acc, kvg, sem_o, sem_s = refs[-8:]
    n_keys, n_rows = crossing(doc, distance)

    def copy_o(h, toks):
        return pltpu.make_async_copy(dq_t.at[h, :, pl.ds(0, toks)], dqt_out.at[h, :, pl.ds(0, toks)], sem_o.at[h])

    def run(keys, toks):
        off = total - keys
        here = slice(off, total)
        key_row = lax.broadcasted_iota(jnp.int32, (keys, DH), 0)
        live = key_row >= keys - n_keys * BLK
        near = k_in[here, :] if distance == 1 else kv_in[here, 0:DH]
        k[0:keys, :] = jnp.where(live, near, jnp.zeros((keys, DH), BF16))
        k_t[:, 0:keys] = jnp.transpose(k[0:keys, :])
        tok_live = lax.broadcasted_iota(jnp.int32, (H, toks), 1) < n_rows * BLK
        ln2[:, 0:toks] = jnp.where(tok_live, ln[:, 0:toks] * LOG2E, -FAR)
        acc[0:keys, :] = jnp.zeros((keys, 2 * DH), F32)

        @pl.loop(0, H, unroll=2)
        def _(h):
            v = v_in[here, :] if distance == 1 else kv_in[here, DH:]
            x, dk, dv = piece(
                k[0:keys, :], v, k_t[:, 0:keys], q[0:toks, cols(h)], g[0:toks, cols(h)],
                ln2[row(h), 0:toks], delta[row(h), 0:toks], None,
            )
            dq_t[h, :, 0:toks] = x
            acc[0:keys, 0:DH] += dk
            acc[0:keys, DH:] += dv
            copy_o(h, toks).start()

        zero = jnp.zeros((keys, DH), F32)
        kvg[here, 0:DH] = jnp.where(live, acc[0:keys, 0:DH] * SCALE, zero).astype(BF16)
        kvg[here, DH:] = jnp.where(live, acc[0:keys, DH:], zero).astype(BF16)
        if off:
            kvg[0:off, :] = jnp.zeros((off, 2 * DH), BF16)
        for h in range(H):
            copy_o(h, toks).wait()

    few_keys = n_keys * BLK <= HALF
    few_rows = n_rows * BLK <= HALF

    @pl.when(n_keys == 0)
    def _():
        kvg[...] = jnp.zeros((total, 2 * DH), BF16)

    for keys in (HALF, total):
        for toks in (HALF, TOK):
            ok = (n_keys > 0) & (few_keys == (keys == HALF)) & (few_rows == (toks == HALF))
            pl.when(ok)(functools.partial(run, keys, toks))
    c = pltpu.make_async_copy(kvg, kvg_out, sem_s.at[0])
    c.start()
    c.wait()


def remote_pieces(distance, doc, q, g, ln_t, delta, *kv):
    total = TOK if distance == 1 else FAR_TOK
    return pl.pallas_call(
        functools.partial(remote_kernel, distance),
        name=f"remote_{distance}",
        out_shape=(
            jax.ShapeDtypeStruct((H, DH, TOK), F32),
            jax.ShapeDtypeStruct((total, 2 * DH), BF16),
        ),
        in_specs=[SMEM] + [VMEM] * (4 + len(kv)),
        out_specs=(ANY, ANY),
        scratch_shapes=[
            pltpu.VMEM((total, DH), BF16),
            pltpu.VMEM((DH, total), BF16),
            pltpu.VMEM((H, TOK), F32),
            pltpu.VMEM((H, DH, TOK), F32),
            pltpu.VMEM((total, 2 * DH), F32),
            pltpu.VMEM((total, 2 * DH), BF16),
            pltpu.SemaphoreType.DMA((H,)),
            pltpu.SemaphoreType.DMA((1,)),
        ],
        compiler_params=pltpu.CompilerParams(vmem_limit_bytes=VMEM_LIMIT),
        cost_estimate=pl.CostEstimate(flops=4_000_000_000, bytes_accessed=6_000_000, transcendentals=2_000_000),
    )(doc, q, g, ln_t, delta, *kv)


def late_kernel(
    doc, q, k, v, g, ln, delta, own_hbm, rem1_hbm, rem2_hbm,
    dq_out, dkv_out,
    k_t, bias, own, rem1, rem2, dq, dkv, sem_i, sem_r, sem_o,
):
    c_own = pltpu.make_async_copy(own_hbm, own.at[pl.ds(0, HEADS_A)], sem_i.at[0])
    c_own.start()
    spans = [crossing(doc, d) for d in (1, 2)]
    rems = (rem1, rem2)
    copies = [pltpu.make_async_copy(src, dst, sem_r.at[m]) for m, (src, dst) in enumerate(((rem1_hbm, rem1), (rem2_hbm, rem2)))]
    for c, (n_keys, _) in zip(copies, spans):
        pl.when(n_keys > 0)(c.start)
    if HEADS_A < H:
        fill_bias(doc, bias)
        k_t[...] = jnp.transpose(k[...])
        dkv[...] = jnp.zeros((TOK, 2 * DH), F32)

        @pl.loop(HEADS_A, H, unroll=2)
        def _(h):
            lo, hi = own_head(
                q[:, cols(h)], g[:, cols(h)], k, v, k_t, ln[row(h), :] * LOG2E, delta[row(h), :], bias, dkv
            )
            own[h, :, 0:HALF] = lo
            own[h, :, HALF:] = hi

        c_dkv = pltpu.make_async_copy(dkv, dkv_out, sem_i.at[1])
        c_dkv.start()
    c_own.wait()
    for c, rem, (n_keys, n_rows) in zip(copies, rems, spans):

        @pl.when(n_keys > 0)
        def _():
            c.wait()
            live = lax.broadcasted_iota(jnp.int32, (DH, TOK), 1) < n_rows * BLK

            @pl.loop(0, H, unroll=2)
            def _(h):
                own[h] += jnp.where(live, rem[h], 0.0)

    def copy_o(h):
        return pltpu.make_async_copy(dq.at[h], dq_out.at[:, cols(h)], sem_o.at[h])

    @pl.loop(0, H, unroll=2)
    def _(h):
        dq[h] = (jnp.transpose(own[h]) * SCALE).astype(BF16)
        copy_o(h).start()

    for h in range(H):
        copy_o(h).wait()
    if HEADS_A < H:
        c_dkv.wait()


def late(doc, q, k, v, g, ln_t, delta, own, rem1, rem2):
    every = pltpu.VMEM((H, DH, TOK), F32)
    return pl.pallas_call(
        late_kernel,
        name="late",
        out_shape=(
            jax.ShapeDtypeStruct((TOK, H * DH), BF16),
            jax.ShapeDtypeStruct((TOK, 2 * DH), F32),
        ),
        in_specs=[SMEM] + [VMEM] * 6 + [ANY] * 3,
        out_specs=(ANY, ANY),
        scratch_shapes=[
            pltpu.VMEM((DH, TOK), BF16),
            pltpu.VMEM((TOK, TOK), F32),
            every, every, every,
            pltpu.VMEM((H, TOK, DH), BF16),
            pltpu.VMEM((TOK, 2 * DH), F32),
            pltpu.SemaphoreType.DMA((2,)),
            pltpu.SemaphoreType.DMA((2,)),
            pltpu.SemaphoreType.DMA((H,)),
        ],
        compiler_params=pltpu.CompilerParams(vmem_limit_bytes=VMEM_LIMIT),
        cost_estimate=pl.CostEstimate(flops=4_000_000_000, bytes_accessed=5_000_000, transcendentals=0),
    )(doc, q, k, v, g, ln_t, delta, own, rem1, rem2)


def moved(value, by):
    count = lax.axis_size("seq")
    return lax.ppermute(value, "seq", [(i, (i + by) % count) for i in range(count)])


def local(queries, key_input, value_input, attn_out, out_grad, log_norm, doc_block):
    ln_t = log_norm.T
    near_k = moved(key_input, 1)
    near_v = moved(value_input, 1)
    delta, dqt, dkv_a, far = early(doc_block, queries, key_input, value_input, attn_out, out_grad, ln_t)
    far = moved(far, 2)
    rem1, part1 = remote_pieces(1, doc_block, queries, out_grad, ln_t, delta, near_k, near_v)
    back1 = moved(part1, -1)
    rem2, part2 = remote_pieces(2, doc_block, queries, out_grad, ln_t, delta, far)
    back2 = moved(part2, -2)
    dq, dkv_b = late(doc_block, queries, key_input, value_input, out_grad, ln_t, delta, dqt, rem1, rem2)
    dkv = dkv_a + dkv_b
    dk = dkv[:, :DH] * SCALE + back1[:, :DH].astype(F32)
    dv = dkv[:, DH:] + back1[:, DH:].astype(F32)
    dk = jnp.concatenate([dk[:BLK], dk[BLK:] + back2[:, :DH].astype(F32)], axis=0)
    dv = jnp.concatenate([dv[:BLK], dv[BLK:] + back2[:, DH:].astype(F32)], axis=0)
    return dq, dk.astype(BF16), dv.astype(BF16)


def solution(mesh):
    return jax.shard_map(
        local,
        mesh=mesh,
        in_specs=(
            P(("dp", "seq"), None),
            P(("dp", "seq"), None),
            P(("dp", "seq"), None),
            P(("dp", "seq"), None),
            P(("dp", "seq"), None),
            P(("dp", "seq"), None),
            P("dp"),
        ),
        out_specs=(P(("dp", "seq"), None), P(("dp", "seq"), None), P(("dp", "seq"), None)),
        check_vma=False,
    )
```

profile of v0, /device:TPU:1, one launch (start us, length us, event | category | flops | bytes accessed | tf_op | source)
XLA Modules:
  0.0 32.9 jit_solution(3990701103013692851)
XLA Ops:
  0.6 2.8 %collective-permute-start = (bf16[512,128]{1,0:T(8,128)(2,1)}, bf16[512,128]{1,0:T(8,128)(2,1)S(1)}, u32[]{:S(2)}, u32[]{:S(2)}) collective-permute-start(bf16[512,128]{1,0:T(8,128)(2,1)} %k.1), channel_id=1, source_target_pairs={{0,4},{4,8},{8,12},{12,16},{16,20},{20,24},{24,28},{28,32},{32,36}... | collective-permute-start | bytes 393224 | tf_op jit(solution)/shard_map/ppermute | solution.py:381
  3.4 0.1 collective-permute-start.1
  3.5 0.0 copy-start
  3.5 0.0 copy-start.1
  3.5 0.0 copy-start.4
  3.5 0.0 copy-start.5
  3.5 8.3 %early.1 = (f32[8,512]{1,0:T(8,128)}, f32[4,128,512]{2,1,0:T(8,128)}, f32[512,256]{1,0:T(8,128)}, bf16[384,256]{1,0:T(8,128)(2,1)}) custom-call(s32[256]{0:T(256)} %doc.3, bf16[512,1024]{1,0:T(8,128)(2,1)} %q.1, bf16[512,128]{1,0:T(8,128)(2,1)} %k.1, bf16[512,128]{1,0:T(8,128)(2,1)} %v.1, bf16[512,1024]{1,0:T(8,128)(2,1)} %a_hbm.1, bf16[512,1024]{1,0:T(8,128)(2,1)} %g.1, ...), custom_call_target="tpu_custom_call" | custom-call | flops 4000000000 | bytes 6000000 | tf_op jit(solution)/shard_map/early/pallas_call | solution.py:180
  11.8 1.4 %collective-permute-start.2 = (bf16[384,256]{1,0:T(8,128)(2,1)}, bf16[384,256]{1,0:T(8,128)(2,1)S(1)}, u32[]{:S(2)}, u32[]{:S(2)}) collective-permute-start(bf16[384,256]{1,0:T(8,128)(2,1)} %get-tuple-element.16), channel_id=1, source_target_pairs={{0,8},{4,12},{8,16},{12,20},{16,24},{20,28},{24,32},{28,36},{32,40... | collective-permute-start | bytes 589832 | tf_op jit(solution)/shard_map/ppermute | solution.py:381
  13.2 0.0 collective-permute-done.refs_5_
  13.2 0.0 collective-permute-done.1.refs_6_
  13.2 0.0 copy-done
  13.2 0.0 copy-done.1
  13.2 0.0 copy-done.4
  13.3 0.0 copy-done.5
  13.3 0.0 copy-start.7
  13.3 0.7 %copy-done.7 = f32[8,512]{1,0:T(8,128)S(1)} copy-done((f32[8,512]{1,0:T(8,128)S(1)}, f32[8,512]{1,0:T(8,128)}, u32[]{:S(2)}) %copy-start.7) | copy-done | bytes 16408
  14.0 0.0 copy-start.8
  14.0 7.4 %remote_1.1 = (f32[8,128,512]{2,1,0:T(8,128)S(1)}, bf16[512,256]{1,0:T(8,128)(2,1)S(1)}) custom-call(s32[256]{0:T(256)S(1)} %copy-done.5, bf16[512,1024]{1,0:T(8,128)(2,1)S(1)} %copy-done, bf16[512,1024]{1,0:T(8,128)(2,1)S(1)} %copy-done.1, f32[8,512]{1,0:T(8,128)S(1)} %bitcast.2, f32[8,512]{1,0:T(8,128)S(1)} %copy-done.7, ...), custom_call_target="tpu_custom_call" | custom-call | flops 4000000000 | bytes 6000000 | tf_op jit(solution)/shard_map/remote_1/pallas_call | solution.py:276
  21.4 0.0 copy-start.2
  21.4 0.0 copy-start.3
  21.4 0.0 copy-start.6
  21.4 0.1 collective-permute-start.3
  21.5 1.5 %collective-permute-done.2.refs_5_ = bf16[384,256]{1,0:T(8,128)(2,1)S(1)} collective-permute-done((bf16[384,256]{1,0:T(8,128)(2,1)}, bf16[384,256]{1,0:T(8,128)(2,1)S(1)}, u32[]{:S(2)}, u32[]{:S(2)}) %collective-permute-start.2) | collective-permute-done | bytes 196640 | tf_op jit(solution)/shard_map/ppermute | solution.py:381
  23.0 0.0 copy-done.8
  23.0 1.1 %remote_2.1 = (f32[8,128,512]{2,1,0:T(8,128)S(1)}, bf16[384,256]{1,0:T(8,128)(2,1)S(1)}) custom-call(s32[256]{0:T(256)S(1)} %copy-done.5, bf16[512,1024]{1,0:T(8,128)(2,1)S(1)} %copy-done, bf16[512,1024]{1,0:T(8,128)(2,1)S(1)} %copy-done.1, f32[8,512]{1,0:T(8,128)S(1)} %bitcast.3, f32[8,512]{1,0:T(8,128)S(1)} %copy-done.8, ...), custom_call_target="tpu_custom_call" | custom-call | flops 4000000000 | bytes 6000000 | tf_op jit(solution)/shard_map/remote_2/pallas_call | solution.py:276
  24.1 2.3 %collective-permute-start.4 = (bf16[384,256]{1,0:T(8,128)(2,1)S(1)}, bf16[384,256]{1,0:T(8,128)(2,1)S(1)}, u32[]{:S(2)}, u32[]{:S(2)}) collective-permute-start(bf16[384,256]{1,0:T(8,128)(2,1)S(1)} %get-tuple-element.22), channel_id=1, source_target_pairs={{0,248},{4,252},{8,0},{12,4},{16,8},{20,12},{24,16},{28,20},{32,24... | collective-permute-start | bytes 589832 | tf_op jit(solution)/shard_map/ppermute | solution.py:381
  26.4 0.0 copy-done.2
  26.4 0.0 copy-done.3
  26.4 0.0 copy-done.6
  26.4 0.0 copy-start.9
  26.5 5.5 %late.1 = (bf16[512,1024]{1,0:T(8,128)(2,1)}, f32[512,256]{1,0:T(8,128)S(1)}) custom-call(s32[256]{0:T(256)S(1)} %copy-done.5, bf16[512,1024]{1,0:T(8,128)(2,1)S(1)} %copy-done, bf16[512,128]{1,0:T(8,128)(2,1)S(1)} %copy-done.2, bf16[512,128]{1,0:T(8,128)(2,1)S(1)} %copy-done.3, bf16[512,1024]{1,0:T(8,128)(2,1)S(1)} %copy-done.1, f32[8,512]{1,0:T(8,128)S(1)} %bitcast.4, ...), custom_call_target="tpu_custom_call" | custom-call | flops 4000000000 | bytes 5000000 | tf_op jit(solution)/shard_map/late/pallas_call | solution.py:355
  31.9 0.0 copy-done.9
  31.9 0.1 add.15
  32.0 0.0 collective-permute-done.3
  32.0 0.1 slice_add_fusion
  32.1 0.0 collective-permute-done.4
  32.2 0.7 %pad_maximum_fusion = (bf16[512,128]{1,0:T(8,128)(2,1)}, bf16[512,128]{1,0:T(8,128)(2,1)}) fusion(bf16[384,128]{1,0:T(8,128)(2,1)S(1)} %get-tuple-element.26, bf16[128,128]{1,0:T(8,128)(2,1)S(1)} %slice.69, bf16[384,128]{1,0:T(8,128)(2,1)S(1)} %get-tuple-element.25, bf16[128,128]{1,0:T(8,128)(2,1)S(1)} %slice.68), kind=kLoop, calls=%fused_computation.7 | loop fusion | flops 524288 | bytes 524288 | tf_op jit(solution)/shard_map/concatenate | solution.py:398
  (3 shorter events, 0.1 us)
Async XLA Ops:
  0.6 12.6 %collective-permute-start = (bf16[512,128]{1,0:T(8,128)(2,1)}, bf16[512,128]{1,0:T(8,128)(2,1)S(1)}, u32[]{:S(2)}, u32[]{:S(2)}) collective-permute-start(bf16[512,128]{1,0:T(8,128)(2,1)} %k.1), channel_id=1, source_target_pairs={{0,4},{4,8},{8,12},{12,16},{16,20},{20,24},{24,28},{28,32},{32,36}... | collective-permute-start | bytes 393224 | tf_op jit(solution)/shard_map/ppermute | solution.py:381
  3.4 9.8 %collective-permute-start.1 = (bf16[512,128]{1,0:T(8,128)(2,1)}, bf16[512,128]{1,0:T(8,128)(2,1)S(1)}, u32[]{:S(2)}, u32[]{:S(2)}) collective-permute-start(bf16[512,128]{1,0:T(8,128)(2,1)} %v.1), channel_id=1, source_target_pairs={{0,4},{4,8},{8,12},{12,16},{16,20},{20,24},{24,28},{28,32},{32,36}... | collective-permute-start | bytes 393224 | tf_op jit(solution)/shard_map/ppermute | solution.py:381
  3.5 9.7 %copy-start = (bf16[512,1024]{1,0:T(8,128)(2,1)S(1)}, bf16[512,1024]{1,0:T(8,128)(2,1)}, u32[]{:S(2)}) copy-start(bf16[512,1024]{1,0:T(8,128)(2,1)} %q.1) | copy-start | bytes 3145732
  3.5 9.7 %copy-start.1 = (bf16[512,1024]{1,0:T(8,128)(2,1)S(1)}, bf16[512,1024]{1,0:T(8,128)(2,1)}, u32[]{:S(2)}) copy-start(bf16[512,1024]{1,0:T(8,128)(2,1)} %g.1) | copy-start | bytes 3145732
  3.5 9.8 %copy-start.4 = (f32[512,8]{0,1:T(8,128)S(1)}, f32[512,8]{0,1:T(8,128)}, u32[]{:S(2)}) copy-start(f32[512,8]{0,1:T(8,128)} %param.12) | copy-start | bytes 49156
  3.5 9.8 %copy-start.5 = (s32[256]{0:T(256)S(1)}, s32[256]{0:T(256)}, u32[]{:S(2)}) copy-start(s32[256]{0:T(256)} %doc.3) | copy-start | bytes 3076
  11.8 11.1 %collective-permute-start.2 = (bf16[384,256]{1,0:T(8,128)(2,1)}, bf16[384,256]{1,0:T(8,128)(2,1)S(1)}, u32[]{:S(2)}, u32[]{:S(2)}) collective-permute-start(bf16[384,256]{1,0:T(8,128)(2,1)} %get-tuple-element.16), channel_id=1, source_target_pairs={{0,8},{4,12},{8,16},{12,20},{16,24},{20,28},{24,32},{28,36},{32,40... | collective-permute-start | bytes 589832 | tf_op jit(solution)/shard_map/ppermute | solution.py:381
  13.3 0.7 %copy-start.7 = (f32[8,512]{1,0:T(8,128)S(1)}, f32[8,512]{1,0:T(8,128)}, u32[]{:S(2)}) copy-start(f32[8,512]{1,0:T(8,128)} %get-tuple-element.13.refs_4_.delta) | copy-start | bytes 49156
  14.0 9.0 %copy-start.8 = (f32[8,512]{1,0:T(8,128)S(1)}, f32[8,512]{1,0:T(8,128)}, u32[]{:S(2)}) copy-start(f32[8,512]{1,0:T(8,128)} %get-tuple-element.13.refs_4_.delta) | copy-start | bytes 49156
  21.4 5.1 %copy-start.2 = (bf16[512,128]{1,0:T(8,128)(2,1)S(1)}, bf16[512,128]{1,0:T(8,128)(2,1)}, u32[]{:S(2)}) copy-start(bf16[512,128]{1,0:T(8,128)(2,1)} %k.1) | copy-start | bytes 393220
  21.4 5.1 %copy-start.3 = (bf16[512,128]{1,0:T(8,128)(2,1)S(1)}, bf16[512,128]{1,0:T(8,128)(2,1)}, u32[]{:S(2)}) copy-start(bf16[512,128]{1,0:T(8,128)(2,1)} %v.1) | copy-start | bytes 393220
  21.4 5.1 %copy-start.6 = (f32[4,128,512]{2,1,0:T(8,128)S(1)}, f32[4,128,512]{2,1,0:T(8,128)}, u32[]{:S(2)}) copy-start(f32[4,128,512]{2,1,0:T(8,128)} %get-tuple-element.14.own_hbm) | copy-start | bytes 3145732
  21.4 10.6 %collective-permute-start.3 = (bf16[512,256]{1,0:T(8,128)(2,1)S(1)}, bf16[512,256]{1,0:T(8,128)(2,1)S(1)}, u32[]{:S(2)}, u32[]{:S(2)}) collective-permute-start(bf16[512,256]{1,0:T(8,128)(2,1)S(1)} %get-tuple-element.21), channel_id=1, source_target_pairs={{0,252},{4,0},{8,4},{12,8},{16,12},{20,16},{24,20},{28,24},{32,28}... | collective-permute-start | bytes 786440 | tf_op jit(solution)/shard_map/ppermute | solution.py:381
  24.1 8.0 %collective-permute-start.4 = (bf16[384,256]{1,0:T(8,128)(2,1)S(1)}, bf16[384,256]{1,0:T(8,128)(2,1)S(1)}, u32[]{:S(2)}, u32[]{:S(2)}) collective-permute-start(bf16[384,256]{1,0:T(8,128)(2,1)S(1)} %get-tuple-element.22), channel_id=1, source_target_pairs={{0,248},{4,252},{8,0},{12,4},{16,8},{20,12},{24,16},{28,20},{32,24... | collective-permute-start | bytes 589832 | tf_op jit(solution)/shard_map/ppermute | solution.py:381
  26.4 5.5 %copy-start.9 = (f32[512,256]{1,0:T(8,128)S(1)}, f32[512,256]{1,0:T(8,128)}, u32[]{:S(2)}) copy-start(f32[512,256]{1,0:T(8,128)} %get-tuple-element.19) | copy-start | bytes 1572868
where the time goes:
time: 33.3 us; the launch traced here: 32.9 us
  Pallas kernels  22.3 us (67%)
  starting transfers between devices  6.65 us (20%)
  waiting for transfers between devices  1.5 us (5%)
  other arithmetic  0.9 us (3%)
  between operations  0.8 us (2%)
  local copies, waits for them, and re-layouts  0.77 us (2%)
    pallas_call x2, Pallas kernels, remote_pieces(): pl.pallas_call(functools.partial(remote_kernel, distance), name=f'remote_...  8.49 us
    pallas_call x1, Pallas kernels, early(): pl.pallas_call(early_kernel, name='early', out_shape=(jax.ShapeDtypeStruc...  8.34 us
    ppermute x5, starting transfers between devices, moved(): lax.ppermute(value, 'seq', [(i, (i + by) % count) for i in range(count)])  6.65 us
    pallas_call x1, Pallas kernels, late(): pl.pallas_call(late_kernel, name='late', out_shape=(jax.ShapeDtypeStruct(...  5.46 us
    ppermute x5, waiting for transfers between devices, moved(): lax.ppermute(value, 'seq', [(i, (i + by) % count) for i in range(count)])  1.5 us
    unnamed x20, local copies, waits for them, and re-layouts  0.75 us
    concatenate x1, other arithmetic, local(): jnp.concatenate([dk[:BLK], dk[BLK:] + back2[:, :DH].astype(F32)], axis=0)  0.72 us
  transfers between devices with their start and end apart: 5, of which 1 were waited for; matrix products, arithmetic and copies ran while one was open for 0% of the time, Pallas kernels for 68%

commit v1 on v0

--- a/solution.py
+++ b/solution.py
@@ -112,8 +112,8 @@
 
 def early_kernel(
     doc, q_hbm, k_hbm, v_hbm, a_hbm, g_hbm, ln_hbm,
-    delta_out, dqt_out, dkv_out, far_out,
-    q, g, a, k, v, k_t, ln, delta, bias, dq_t, dkv, far, sem_q, sem_g, sem_a, sem_s, sem_o,
+    delta_out, dqt_out, dkv_out,
+    q, g, a, k, v, k_t, ln, delta, bias, dq_t, dkv, sem_q, sem_g, sem_a, sem_s, sem_o,
 ):
     small = [
         pltpu.make_async_copy(k_hbm, k, sem_s.at[0]),
@@ -145,8 +145,6 @@
     for c in small:
         c.wait()
     k_t[...] = jnp.transpose(k[...])
-    far[:, 0:DH] = k[BLK:, :]
-    far[:, DH:] = v[BLK:, :]
 
     @pl.loop(0, H, unroll=2)
     def _(h):
@@ -165,7 +163,6 @@
     tail = [
         pltpu.make_async_copy(delta, delta_out, sem_s.at[0]),
         pltpu.make_async_copy(dkv, dkv_out, sem_s.at[1]),
-        pltpu.make_async_copy(far, far_out, sem_s.at[2]),
     ]
     for c in tail:
         c.start()
@@ -184,10 +181,9 @@
             jax.ShapeDtypeStruct((H, TOK), F32),
             jax.ShapeDtypeStruct((HEADS_A, DH, TOK), F32),
             jax.ShapeDtypeStruct((TOK, 2 * DH), F32),
-            jax.ShapeDtypeStruct((FAR_TOK, 2 * DH), BF16),
         ),
         in_specs=[SMEM] + [ANY] * 6,
-        out_specs=(ANY,) * 4,
+        out_specs=(ANY,) * 3,
         scratch_shapes=[
             big, big, big,
             pltpu.VMEM((TOK, DH), BF16),
@@ -198,7 +194,6 @@
             pltpu.VMEM((TOK, TOK), F32),
             pltpu.VMEM((HEADS_A, DH, TOK), F32),
             pltpu.VMEM((TOK, 2 * DH), F32),
-            pltpu.VMEM((FAR_TOK, 2 * DH), BF16),
             pltpu.SemaphoreType.DMA((H,)),
             pltpu.SemaphoreType.DMA((H,)),
             pltpu.SemaphoreType.DMA((H,)),
@@ -210,148 +205,168 @@
     )(doc, q, k, v, a, g, ln_t)
 
 
-def remote_kernel(distance, *refs):
-    if distance == 1:
-        doc, q, g, ln, delta, k_in, v_in, dqt_out, kvg_out = refs[:9]
-        total = TOK
-    else:
-        doc, q, g, ln, delta, kv_in, dqt_out, kvg_out = refs[:8]
-        total = FAR_TOK
-    k, k_t, ln2, dq_t, acc, kvg, sem_o, sem_s = refs[-8:]
-    n_keys, n_rows = crossing(doc, distance)
+def remote_kernel(
+    doc, q, g, ln, delta_hbm, k1, v1, k2, v2,
+    dqt_out, near_out, far_out,
+    delta, k, k_t, ln2, dq_t, acc, near, far, sem_o, sem_s,
+):
+    c_delta = pltpu.make_async_copy(delta_hbm, delta, sem_s.at[0])
+    c_delta.start()
+    n_keys, n_rows = crossing(doc, 1)
+    n_far, _ = crossing(doc, 2)
 
     def copy_o(h, toks):
         return pltpu.make_async_copy(dq_t.at[h, :, pl.ds(0, toks)], dqt_out.at[h, :, pl.ds(0, toks)], sem_o.at[h])
 
-    def run(keys, toks):
-        off = total - keys
-        here = slice(off, total)
-        key_row = lax.broadcasted_iota(jnp.int32, (keys, DH), 0)
-        live = key_row >= keys - n_keys * BLK
-        near = k_in[here, :] if distance == 1 else kv_in[here, 0:DH]
-        k[0:keys, :] = jnp.where(live, near, jnp.zeros((keys, DH), BF16))
-        k_t[:, 0:keys] = jnp.transpose(k[0:keys, :])
+    def mask_rows(toks):
         tok_live = lax.broadcasted_iota(jnp.int32, (H, toks), 1) < n_rows * BLK
         ln2[:, 0:toks] = jnp.where(tok_live, ln[:, 0:toks] * LOG2E, -FAR)
+
+    def load_keys(k_in, v_in, keys, count):
+        here = slice(TOK - keys, TOK)
+        key_row = lax.broadcasted_iota(jnp.int32, (keys, DH), 0)
+        live = key_row >= keys - count * BLK
+        k[0:keys, :] = jnp.where(live, k_in[here, :], jnp.zeros((keys, DH), BF16))
+        k_t[:, 0:keys] = jnp.transpose(k[0:keys, :])
         acc[0:keys, :] = jnp.zeros((keys, 2 * DH), F32)
+        return here, live
+
+    def head(h, v, keys, toks):
+        x, dk, dv = piece(
+            k[0:keys, :], v, k_t[:, 0:keys], q[0:toks, cols(h)], g[0:toks, cols(h)],
+            ln2[row(h), 0:toks], delta[row(h), 0:toks], None,
+        )
+        acc[0:keys, 0:DH] += dk
+        acc[0:keys, DH:] += dv
+        return x
+
+    def store_keys(out, keys, total, live):
+        zero = jnp.zeros((keys, DH), F32)
+        here = slice(total - keys, total)
+        out[here, 0:DH] = jnp.where(live, acc[0:keys, 0:DH] * SCALE, zero).astype(BF16)
+        out[here, DH:] = jnp.where(live, acc[0:keys, DH:], zero).astype(BF16)
+        if keys < total:
+            out[0 : total - keys, :] = jnp.zeros((total - keys, 2 * DH), BF16)
+
+    def run(keys, toks):
+        here, live = load_keys(k1, v1, keys, n_keys)
+        mask_rows(toks)
 
         @pl.loop(0, H, unroll=2)
         def _(h):
-            v = v_in[here, :] if distance == 1 else kv_in[here, DH:]
-            x, dk, dv = piece(
-                k[0:keys, :], v, k_t[:, 0:keys], q[0:toks, cols(h)], g[0:toks, cols(h)],
-                ln2[row(h), 0:toks], delta[row(h), 0:toks], None,
-            )
-            dq_t[h, :, 0:toks] = x
-            acc[0:keys, 0:DH] += dk
-            acc[0:keys, DH:] += dv
-            copy_o(h, toks).start()
-
-        zero = jnp.zeros((keys, DH), F32)
-        kvg[here, 0:DH] = jnp.where(live, acc[0:keys, 0:DH] * SCALE, zero).astype(BF16)
-        kvg[here, DH:] = jnp.where(live, acc[0:keys, DH:], zero).astype(BF16)
-        if off:
-            kvg[0:off, :] = jnp.zeros((off, 2 * DH), BF16)
-        for h in range(H):
-            copy_o(h, toks).wait()
+            dq_t[h, :, 0:toks] = head(h, v1[here, :], keys, toks)
+
+        store_keys(near, keys, TOK, live)
+
+    def run_far():
+        here, live = load_keys(k2, v2, FAR_TOK, n_far)
+        mask_rows(TOK)
+
+        @pl.loop(0, H)
+        def _(h):
+            x = head(h, v2[here, :], FAR_TOK, TOK)
+            tok_live = lax.broadcasted_iota(jnp.int32, (DH, TOK), 1) < n_rows * BLK
+            dq_t[h] = jnp.where(tok_live, dq_t[h] + x, 0.0)
+
+        store_keys(far, FAR_TOK, FAR_TOK, live)
 
     few_keys = n_keys * BLK <= HALF
     few_rows = n_rows * BLK <= HALF
 
     @pl.when(n_keys == 0)
     def _():
-        kvg[...] = jnp.zeros((total, 2 * DH), BF16)
-
-    for keys in (HALF, total):
+        near[...] = jnp.zeros((TOK, 2 * DH), BF16)
+
+    @pl.when(n_far == 0)
+    def _():
+        far[...] = jnp.zeros((FAR_TOK, 2 * DH), BF16)
+
+    c_delta.wait()
+    for keys in (HALF, TOK):
         for toks in (HALF, TOK):
             ok = (n_keys > 0) & (few_keys == (keys == HALF)) & (few_rows == (toks == HALF))
             pl.when(ok)(functools.partial(run, keys, toks))
-    c = pltpu.make_async_copy(kvg, kvg_out, sem_s.at[0])
-    c.start()
-    c.wait()
-
-
-def remote_pieces(distance, doc, q, g, ln_t, delta, *kv):
-    total = TOK if distance == 1 else FAR_TOK
+    pl.when(n_far > 0)(run_far)
+    tail = [
+        pltpu.make_async_copy(near, near_out, sem_s.at[0]),
+        pltpu.make_async_copy(far, far_out, sem_s.at[1]),
+    ]
+    for c in tail:
+        c.start()
+    c_dq = pltpu.make_async_copy(dq_t, dqt_out, sem_o.at[0])
+
+    @pl.when(n_keys > 0)
+    def _():
+        c_dq.start()
+        c_dq.wait()
+
+    for c in tail:
+        c.wait()
+
+
+def remote_pieces(doc, q, g, ln_t, delta, k1, v1, k2, v2):
     return pl.pallas_call(
-        functools.partial(remote_kernel, distance),
-        name=f"remote_{distance}",
+        remote_kernel,
+        name="remote",
         out_shape=(
             jax.ShapeDtypeStruct((H, DH, TOK), F32),
-            jax.ShapeDtypeStruct((total, 2 * DH), BF16),
+            jax.ShapeDtypeStruct((TOK, 2 * DH), BF16),
+            jax.ShapeDtypeStruct((FAR_TOK, 2 * DH), BF16),
         ),
-        in_specs=[SMEM] + [VMEM] * (4 + len(kv)),
-        out_specs=(ANY, ANY),
+        in_specs=[SMEM] + [VMEM] * 3 + [ANY] + [VMEM] * 4,
+        out_specs=(ANY, ANY, ANY),
         scratch_shapes=[
-            pltpu.VMEM((total, DH), BF16),
-            pltpu.VMEM((DH, total), BF16),
+            pltpu.VMEM((H, TOK), F32),
+            pltpu.VMEM((TOK, DH), BF16),
+            pltpu.VMEM((DH, TOK), BF16),
             pltpu.VMEM((H, TOK), F32),
             pltpu.VMEM((H, DH, TOK), F32),
-            pltpu.VMEM((total, 2 * DH), F32),
-            pltpu.VMEM((total, 2 * DH), BF16),
-            pltpu.SemaphoreType.DMA((H,)),
+            pltpu.VMEM((TOK, 2 * DH), F32),
+            pltpu.VMEM((TOK, 2 * DH), BF16),
+            pltpu.VMEM((FAR_TOK, 2 * DH), BF16),
             pltpu.SemaphoreType.DMA((1,)),
+            pltpu.SemaphoreType.DMA((2,)),
         ],
         compiler_params=pltpu.CompilerParams(vmem_limit_bytes=VMEM_LIMIT),
         cost_estimate=pl.CostEstimate(flops=4_000_000_000, bytes_accessed=6_000_000, transcendentals=2_000_000),
-    )(doc, q, g, ln_t, delta, *kv)
+    )(doc, q, g, ln_t, delta, k1, v1, k2, v2)
 
 
 def late_kernel(
-    doc, q, k, v, g, ln, delta, own_hbm, rem1_hbm, rem2_hbm,
+    doc, q, k, v, g, ln, delta, own_a, rem,
     dq_out, dkv_out,
-    k_t, bias, own, rem1, rem2, dq, dkv, sem_i, sem_r, sem_o,
+    k_t, bias, dq, dkv, sem_s, sem_o,
 ):
-    c_own = pltpu.make_async_copy(own_hbm, own.at[pl.ds(0, HEADS_A)], sem_i.at[0])
-    c_own.start()
-    spans = [crossing(doc, d) for d in (1, 2)]
-    rems = (rem1, rem2)
-    copies = [pltpu.make_async_copy(src, dst, sem_r.at[m]) for m, (src, dst) in enumerate(((rem1_hbm, rem1), (rem2_hbm, rem2)))]
-    for c, (n_keys, _) in zip(copies, spans):
-        pl.when(n_keys > 0)(c.start)
-    if HEADS_A < H:
-        fill_bias(doc, bias)
-        k_t[...] = jnp.transpose(k[...])
-        dkv[...] = jnp.zeros((TOK, 2 * DH), F32)
-
-        @pl.loop(HEADS_A, H, unroll=2)
-        def _(h):
-            lo, hi = own_head(
-                q[:, cols(h)], g[:, cols(h)], k, v, k_t, ln[row(h), :] * LOG2E, delta[row(h), :], bias, dkv
-            )
-            own[h, :, 0:HALF] = lo
-            own[h, :, HALF:] = hi
-
-        c_dkv = pltpu.make_async_copy(dkv, dkv_out, sem_i.at[1])
-        c_dkv.start()
-    c_own.wait()
-    for c, rem, (n_keys, n_rows) in zip(copies, rems, spans):
-
-        @pl.when(n_keys > 0)
-        def _():
-            c.wait()
-            live = lax.broadcasted_iota(jnp.int32, (DH, TOK), 1) < n_rows * BLK
-
-            @pl.loop(0, H, unroll=2)
-            def _(h):
-                own[h] += jnp.where(live, rem[h], 0.0)
+    _, n_rows = crossing(doc, 1)
+    fill_bias(doc, bias)
+    k_t[...] = jnp.transpose(k[...])
+    dkv[...] = jnp.zeros((TOK, 2 * DH), F32)
 
     def copy_o(h):
         return pltpu.make_async_copy(dq.at[h], dq_out.at[:, cols(h)], sem_o.at[h])
 
-    @pl.loop(0, H, unroll=2)
+    def finish(h, own):
+        live = lax.broadcasted_iota(jnp.int32, (DH, TOK), 1) < n_rows * BLK
+        full = own + jnp.where(live, rem[h], 0.0)
+        dq[h] = (jnp.transpose(full) * SCALE).astype(BF16)
+        copy_o(h).start()
+
+    @pl.loop(HEADS_A, H, unroll=2)
     def _(h):
-        dq[h] = (jnp.transpose(own[h]) * SCALE).astype(BF16)
-        copy_o(h).start()
-
+        lo, hi = own_head(
+            q[:, cols(h)], g[:, cols(h)], k, v, k_t, ln[row(h), :] * LOG2E, delta[row(h), :], bias, dkv
+        )
+        finish(h - HEADS_A, own_a[h - HEADS_A])
+        finish(h, jnp.concatenate([lo, hi], axis=1))
+
+    c_dkv = pltpu.make_async_copy(dkv, dkv_out, sem_s.at[0])
+    c_dkv.start()
     for h in range(H):
         copy_o(h).wait()
-    if HEADS_A < H:
-        c_dkv.wait()
-
-
-def late(doc, q, k, v, g, ln_t, delta, own, rem1, rem2):
-    every = pltpu.VMEM((H, DH, TOK), F32)
+    c_dkv.wait()
+
+
+def late(doc, q, k, v, g, ln_t, delta, own, rem):
     return pl.pallas_call(
         late_kernel,
         name="late",
@@ -359,21 +374,19 @@
             jax.ShapeDtypeStruct((TOK, H * DH), BF16),
             jax.ShapeDtypeStruct((TOK, 2 * DH), F32),
         ),
-        in_specs=[SMEM] + [VMEM] * 6 + [ANY] * 3,
+        in_specs=[SMEM] + [VMEM] * 8,
         out_specs=(ANY, ANY),
         scratch_shapes=[
             pltpu.VMEM((DH, TOK), BF16),
             pltpu.VMEM((TOK, TOK), F32),
-            every, every, every,
             pltpu.VMEM((H, TOK, DH), BF16),
             pltpu.VMEM((TOK, 2 * DH), F32),
-            pltpu.SemaphoreType.DMA((2,)),
-            pltpu.SemaphoreType.DMA((2,)),
+            pltpu.SemaphoreType.DMA((1,)),
             pltpu.SemaphoreType.DMA((H,)),
         ],
         compiler_params=pltpu.CompilerParams(vmem_limit_bytes=VMEM_LIMIT),
         cost_estimate=pl.CostEstimate(flops=4_000_000_000, bytes_accessed=5_000_000, transcendentals=0),
-    )(doc, q, k, v, g, ln_t, delta, own, rem1, rem2)
+    )(doc, q, k, v, g, ln_t, delta, own, rem)
 
 
 def moved(value, by):
@@ -385,13 +398,13 @@
     ln_t = log_norm.T
     near_k = moved(key_input, 1)
     near_v = moved(value_input, 1)
-    delta, dqt, dkv_a, far = early(doc_block, queries, key_input, value_input, attn_out, out_grad, ln_t)
-    far = moved(far, 2)
-    rem1, part1 = remote_pieces(1, doc_block, queries, out_grad, ln_t, delta, near_k, near_v)
+    far_k = moved(key_input, 2)
+    far_v = moved(value_input, 2)
+    delta, dqt, dkv_a = early(doc_block, queries, key_input, value_input, attn_out, out_grad, ln_t)
+    rem, part1, part2 = remote_pieces(doc_block, queries, out_grad, ln_t, delta, near_k, near_v, far_k, far_v)
     back1 = moved(part1, -1)
-    rem2, part2 = remote_pieces(2, doc_block, queries, out_grad, ln_t, delta, far)
     back2 = moved(part2, -2)
-    dq, dkv_b = late(doc_block, queries, key_input, value_input, out_grad, ln_t, delta, dqt, rem1, rem2)
+    dq, dkv_b = late(doc_block, queries, key_input, value_input, out_grad, ln_t, delta, dqt, rem)
     dkv = dkv_a + dkv_b
     dk = dkv[:, :DH] * SCALE + back1[:, :DH].astype(F32)
     dv = dkv[:, DH:] + back1[:, DH:].astype(F32)

time: 33.3 us -> 35.3 us (1.060)
  waiting for transfers between devices: 1.5 us -> 7.62 us
  Pallas kernels: 22.3 us -> 19.5 us
  starting transfers between devices: 6.65 us -> 5.6 us
    ppermute x5 -> x6, waiting for transfers between devices: 1.5 us -> 7.62 us  [moved(): lax.ppermute(value, 'seq', [(i, (i + by) % count) for i in range(count)])]
    pallas_call x2 -> x1, Pallas kernels: 8.49 us -> 6.92 us  [remote_pieces(): pl.pallas_call(remote_kernel, name='remote', out_shape=(jax.ShapeDtypeStr...]
    pallas_call x1, Pallas kernels: 5.46 us -> 4.29 us  [late(): pl.pallas_call(late_kernel, name='late', out_shape=(jax.ShapeDtypeStruct(...]
    ppermute x5 -> x6, starting transfers between devices: 6.65 us -> 5.6 us  [moved(): lax.ppermute(value, 'seq', [(i, (i + by) % count) for i in range(count)])]
    unnamed x20 -> x18, local copies, waits for them, and re-layouts: 0.75 us -> 0.74 us
  transfers between devices with their start and end apart: 5 -> 6, of which waited for: 1 -> 3; matrix products, arithmetic and copies ran while one was open for 0% -> 0% of each run, Pallas kernels for 68% -> 36%
where the time goes in v1:
time: 35.3 us; the launch traced here: 35.1 us
  Pallas kernels  19.5 us (55%)
  waiting for transfers between devices  7.62 us (22%)
  starting transfers between devices  5.6 us (16%)
  other arithmetic  0.9 us (3%)
  between operations  0.78 us (2%)
  local copies, waits for them, and re-layouts  0.76 us (2%)
    pallas_call x1, Pallas kernels, early(): pl.pallas_call(early_kernel, name='early', out_shape=(jax.ShapeDtypeStruc...  8.25 us
    ppermute x6, waiting for transfers between devices, moved(): lax.ppermute(value, 'seq', [(i, (i + by) % count) for i in range(count)])  7.62 us
    pallas_call x1, Pallas kernels, remote_pieces(): pl.pallas_call(remote_kernel, name='remote', out_shape=(jax.ShapeDtypeStr...  6.92 us
    ppermute x6, starting transfers between devices, moved(): lax.ppermute(value, 'seq', [(i, (i + by) % count) for i in range(count)])  5.6 us
    pallas_call x1, Pallas kernels, late(): pl.pallas_call(late_kernel, name='late', out_shape=(jax.ShapeDtypeStruct(...  4.29 us
    unnamed x18, local copies, waits for them, and re-layouts  0.74 us
    concatenate x1, other arithmetic, local(): jnp.concatenate([dk[:BLK], dk[BLK:] + back2[:, :DH].astype(F32)], axis=0)  0.72 us
  transfers between devices with their start and end apart: 6, of which 3 were waited for; matrix products, arithmetic and copies ran while one was open for 0% of the time, Pallas kernels for 36%

profile of v1, /device:TPU:1, one launch (start us, length us, event | category | flops | bytes accessed | tf_op | source)
XLA Modules:
  0.0 35.1 jit_solution(1052831474694183560)
XLA Ops:
  0.6 2.8 %collective-permute-start = (bf16[512,128]{1,0:T(8,128)(2,1)}, bf16[512,128]{1,0:T(8,128)(2,1)S(1)}, u32[]{:S(2)}, u32[]{:S(2)}) collective-permute-start(bf16[512,128]{1,0:T(8,128)(2,1)} %k.1), channel_id=1, source_target_pairs={{0,4},{4,8},{8,12},{12,16},{16,20},{20,24},{24,28},{28,32},{32,36}... | collective-permute-start | bytes 393224 | tf_op jit(solution)/shard_map/ppermute | solution.py:394
  3.4 1.3 %collective-permute-start.2 = (bf16[512,128]{1,0:T(8,128)(2,1)}, bf16[512,128]{1,0:T(8,128)(2,1)S(1)}, u32[]{:S(2)}, u32[]{:S(2)}) collective-permute-start(bf16[512,128]{1,0:T(8,128)(2,1)} %k.1), channel_id=1, source_target_pairs={{0,8},{4,12},{8,16},{12,20},{16,24},{20,28},{24,32},{28,36},{32,40... | collective-permute-start | bytes 393224 | tf_op jit(solution)/shard_map/ppermute | solution.py:394
  4.7 0.4 %collective-permute-start.1 = (bf16[512,128]{1,0:T(8,128)(2,1)}, bf16[512,128]{1,0:T(8,128)(2,1)S(1)}, u32[]{:S(2)}, u32[]{:S(2)}) collective-permute-start(bf16[512,128]{1,0:T(8,128)(2,1)} %v.1), channel_id=1, source_target_pairs={{0,4},{4,8},{8,12},{12,16},{16,20},{20,24},{24,28},{28,32},{32,36}... | collective-permute-start | bytes 393224 | tf_op jit(solution)/shard_map/ppermute | solution.py:394
  5.1 1.0 %collective-permute-start.3 = (bf16[512,128]{1,0:T(8,128)(2,1)}, bf16[512,128]{1,0:T(8,128)(2,1)S(1)}, u32[]{:S(2)}, u32[]{:S(2)}) collective-permute-start(bf16[512,128]{1,0:T(8,128)(2,1)} %v.1), channel_id=1, source_target_pairs={{0,8},{4,12},{8,16},{12,20},{16,24},{20,28},{24,32},{28,36},{32,40... | collective-permute-start | bytes 393224 | tf_op jit(solution)/shard_map/ppermute | solution.py:394
  6.1 0.0 copy-start
  6.1 0.0 copy-start.1
  6.1 0.0 copy-start.4
  6.1 0.0 copy-start.5
  6.1 8.2 %early.1 = (f32[8,512]{1,0:T(8,128)}, f32[4,128,512]{2,1,0:T(8,128)}, f32[512,256]{1,0:T(8,128)}) custom-call(s32[256]{0:T(256)} %doc.5, bf16[512,1024]{1,0:T(8,128)(2,1)} %q.3, bf16[512,128]{1,0:T(8,128)(2,1)} %k.1, bf16[512,128]{1,0:T(8,128)(2,1)} %v.1, bf16[512,1024]{1,0:T(8,128)(2,1)} %a_hbm.1, bf16[512,1024]{1,0:T(8,128)(2,1)} %g.3, f32[8,512]{1,0:T(8,128)} %bitcast.1), custom_call_target="tpu_custom_call" | custom-call | flops 4000000000 | bytes 6000000 | tf_op jit(solution)/shard_map/early/pallas_call | solution.py:177
  14.3 0.0 collective-permute-done.k1
  14.3 1.4 %collective-permute-done.2.k2 = bf16[512,128]{1,0:T(8,128)(2,1)S(1)} collective-permute-done((bf16[512,128]{1,0:T(8,128)(2,1)}, bf16[512,128]{1,0:T(8,128)(2,1)S(1)}, u32[]{:S(2)}, u32[]{:S(2)}) %collective-permute-start.2) | collective-permute-done | bytes 131104 | tf_op jit(solution)/shard_map/ppermute | solution.py:394
  15.7 0.0 collective-permute-done.1.v1
  15.7 3.4 %collective-permute-done.3.v2 = bf16[512,128]{1,0:T(8,128)(2,1)S(1)} collective-permute-done((bf16[512,128]{1,0:T(8,128)(2,1)}, bf16[512,128]{1,0:T(8,128)(2,1)S(1)}, u32[]{:S(2)}, u32[]{:S(2)}) %collective-permute-start.3) | collective-permute-done | bytes 131104 | tf_op jit(solution)/shard_map/ppermute | solution.py:394
  19.2 0.0 copy-done
  19.2 0.0 copy-done.1
  19.2 0.0 copy-done.4
  19.2 0.0 copy-done.5
  19.2 0.0 copy-start.7
  19.2 0.7 %copy-done.7 = f32[8,512]{1,0:T(8,128)S(1)} copy-done((f32[8,512]{1,0:T(8,128)S(1)}, f32[8,512]{1,0:T(8,128)}, u32[]{:S(2)}) %copy-start.7) | copy-done | bytes 16408
  19.9 0.0 copy-start.2
  19.9 0.0 copy-start.3
  19.9 0.0 copy-start.6
  19.9 6.9 %remote.1 = (f32[8,128,512]{2,1,0:T(8,128)S(1)}, bf16[512,256]{1,0:T(8,128)(2,1)S(1)}, bf16[384,256]{1,0:T(8,128)(2,1)S(1)}) custom-call(s32[256]{0:T(256)S(1)} %copy-done.5, bf16[512,1024]{1,0:T(8,128)(2,1)S(1)} %copy-done, bf16[512,1024]{1,0:T(8,128)(2,1)S(1)} %copy-done.1, f32[8,512]{1,0:T(8,128)S(1)} %bitcast.2, f32[8,512]{1,0:T(8,128)S(1)} %copy-done.7, ...), custom_call_target="tpu_custom_call" | custom-call | flops 4000000000 | bytes 6000000 | tf_op jit(solution)/shard_map/remote/pallas_call | solution.py:308
  26.8 0.1 collective-permute-start.5
  26.9 0.1 collective-permute-start.4
  27.0 0.0 copy-done.2
  27.0 0.0 copy-done.3
  27.0 0.0 copy-done.6
  27.0 0.0 copy-start.8
  27.1 4.3 %late.1 = (bf16[512,1024]{1,0:T(8,128)(2,1)}, f32[512,256]{1,0:T(8,128)S(1)}) custom-call(s32[256]{0:T(256)S(1)} %copy-done.5, bf16[512,1024]{1,0:T(8,128)(2,1)S(1)} %copy-done, bf16[512,128]{1,0:T(8,128)(2,1)S(1)} %copy-done.2, bf16[512,128]{1,0:T(8,128)(2,1)S(1)} %copy-done.3, bf16[512,1024]{1,0:T(8,128)(2,1)S(1)} %copy-done.1, f32[8,512]{1,0:T(8,128)S(1)} %bitcast.3, ...), custom_call_target="tpu_custom_call" | custom-call | flops 4000000000 | bytes 5000000 | tf_op jit(solution)/shard_map/late/pallas_call | solution.py:370
  31.3 0.0 copy-done.8
  31.4 0.1 add.15
  31.4 2.8 %collective-permute-done.4 = bf16[512,256]{1,0:T(8,128)(2,1)S(1)} collective-permute-done((bf16[512,256]{1,0:T(8,128)(2,1)S(1)}, bf16[512,256]{1,0:T(8,128)(2,1)S(1)}, u32[]{:S(2)}, u32[]{:S(2)}) %collective-permute-start.4) | collective-permute-done | bytes 262176 | tf_op jit(solution)/shard_map/ppermute | solution.py:394
  34.2 0.1 slice_add_fusion
  34.3 0.0 collective-permute-done.5
  34.4 0.7 %pad_maximum_fusion = (bf16[512,128]{1,0:T(8,128)(2,1)}, bf16[512,128]{1,0:T(8,128)(2,1)}) fusion(bf16[384,128]{1,0:T(8,128)(2,1)S(1)} %get-tuple-element.22, bf16[128,128]{1,0:T(8,128)(2,1)S(1)} %slice.69, bf16[384,128]{1,0:T(8,128)(2,1)S(1)} %get-tuple-element.21, bf16[128,128]{1,0:T(8,128)(2,1)S(1)} %slice.68), kind=kLoop, calls=%fused_computation.7 | loop fusion | flops 524288 | bytes 524288 | tf_op jit(solution)/shard_map/concatenate | solution.py:411
  (3 shorter events, 0.1 us)
Async XLA Ops:
  0.6 13.7 %collective-permute-start = (bf16[512,128]{1,0:T(8,128)(2,1)}, bf16[512,128]{1,0:T(8,128)(2,1)S(1)}, u32[]{:S(2)}, u32[]{:S(2)}) collective-permute-start(bf16[512,128]{1,0:T(8,128)(2,1)} %k.1), channel_id=1, source_target_pairs={{0,4},{4,8},{8,12},{12,16},{16,20},{20,24},{24,28},{28,32},{32,36}... | collective-permute-start | bytes 393224 | tf_op jit(solution)/shard_map/ppermute | solution.py:394
  3.4 12.3 %collective-permute-start.2 = (bf16[512,128]{1,0:T(8,128)(2,1)}, bf16[512,128]{1,0:T(8,128)(2,1)S(1)}, u32[]{:S(2)}, u32[]{:S(2)}) collective-permute-start(bf16[512,128]{1,0:T(8,128)(2,1)} %k.1), channel_id=1, source_target_pairs={{0,8},{4,12},{8,16},{12,20},{16,24},{20,28},{24,32},{28,36},{32,40... | collective-permute-start | bytes 393224 | tf_op jit(solution)/shard_map/ppermute | solution.py:394
  4.7 11.0 %collective-permute-start.1 = (bf16[512,128]{1,0:T(8,128)(2,1)}, bf16[512,128]{1,0:T(8,128)(2,1)S(1)}, u32[]{:S(2)}, u32[]{:S(2)}) collective-permute-start(bf16[512,128]{1,0:T(8,128)(2,1)} %v.1), channel_id=1, source_target_pairs={{0,4},{4,8},{8,12},{12,16},{16,20},{20,24},{24,28},{28,32},{32,36}... | collective-permute-start | bytes 393224 | tf_op jit(solution)/shard_map/ppermute | solution.py:394
  5.1 14.1 %collective-permute-start.3 = (bf16[512,128]{1,0:T(8,128)(2,1)}, bf16[512,128]{1,0:T(8,128)(2,1)S(1)}, u32[]{:S(2)}, u32[]{:S(2)}) collective-permute-start(bf16[512,128]{1,0:T(8,128)(2,1)} %v.1), channel_id=1, source_target_pairs={{0,8},{4,12},{8,16},{12,20},{16,24},{20,28},{24,32},{28,36},{32,40... | collective-permute-start | bytes 393224 | tf_op jit(solution)/shard_map/ppermute | solution.py:394
  6.1 13.1 %copy-start = (bf16[512,1024]{1,0:T(8,128)(2,1)S(1)}, bf16[512,1024]{1,0:T(8,128)(2,1)}, u32[]{:S(2)}) copy-start(bf16[512,1024]{1,0:T(8,128)(2,1)} %q.3) | copy-start | bytes 3145732
  6.1 13.1 %copy-start.1 = (bf16[512,1024]{1,0:T(8,128)(2,1)S(1)}, bf16[512,1024]{1,0:T(8,128)(2,1)}, u32[]{:S(2)}) copy-start(bf16[512,1024]{1,0:T(8,128)(2,1)} %g.3) | copy-start | bytes 3145732
  6.1 13.1 %copy-start.4 = (f32[512,8]{0,1:T(8,128)S(1)}, f32[512,8]{0,1:T(8,128)}, u32[]{:S(2)}) copy-start(f32[512,8]{0,1:T(8,128)} %param.12) | copy-start | bytes 49156
  6.1 13.1 %copy-start.5 = (s32[256]{0:T(256)S(1)}, s32[256]{0:T(256)}, u32[]{:S(2)}) copy-start(s32[256]{0:T(256)} %doc.5) | copy-start | bytes 3076
  19.2 0.7 %copy-start.7 = (f32[8,512]{1,0:T(8,128)S(1)}, f32[8,512]{1,0:T(8,128)}, u32[]{:S(2)}) copy-start(f32[8,512]{1,0:T(8,128)} %get-tuple-element.11.delta_hbm.delta) | copy-start | bytes 49156
  19.9 7.1 %copy-start.2 = (bf16[512,128]{1,0:T(8,128)(2,1)S(1)}, bf16[512,128]{1,0:T(8,128)(2,1)}, u32[]{:S(2)}) copy-start(bf16[512,128]{1,0:T(8,128)(2,1)} %k.1) | copy-start | bytes 393220
  19.9 7.1 %copy-start.3 = (bf16[512,128]{1,0:T(8,128)(2,1)S(1)}, bf16[512,128]{1,0:T(8,128)(2,1)}, u32[]{:S(2)}) copy-start(bf16[512,128]{1,0:T(8,128)(2,1)} %v.1) | copy-start | bytes 393220
  19.9 7.1 %copy-start.6 = (f32[4,128,512]{2,1,0:T(8,128)S(1)}, f32[4,128,512]{2,1,0:T(8,128)}, u32[]{:S(2)}) copy-start(f32[4,128,512]{2,1,0:T(8,128)} %get-tuple-element.12.own_a) | copy-start | bytes 3145732
  26.8 7.5 %collective-permute-start.5 = (bf16[384,256]{1,0:T(8,128)(2,1)S(1)}, bf16[384,256]{1,0:T(8,128)(2,1)S(1)}, u32[]{:S(2)}, u32[]{:S(2)}) collective-permute-start(bf16[384,256]{1,0:T(8,128)(2,1)S(1)} %get-tuple-element.18), channel_id=1, source_target_pairs={{0,248},{4,252},{8,0},{12,4},{16,8},{20,12},{24,16},{28,20},{32,24... | collective-permute-start | bytes 589832 | tf_op jit(solution)/shard_map/ppermute | solution.py:394
  26.9 7.3 %collective-permute-start.4 = (bf16[512,256]{1,0:T(8,128)(2,1)S(1)}, bf16[512,256]{1,0:T(8,128)(2,1)S(1)}, u32[]{:S(2)}, u32[]{:S(2)}) collective-permute-start(bf16[512,256]{1,0:T(8,128)(2,1)S(1)} %get-tuple-element.17), channel_id=1, source_target_pairs={{0,252},{4,0},{8,4},{12,8},{16,12},{20,16},{24,20},{28,24},{32,28}... | collective-permute-start | bytes 786440 | tf_op jit(solution)/shard_map/ppermute | solution.py:394
  27.0 4.3 %copy-start.8 = (f32[512,256]{1,0:T(8,128)S(1)}, f32[512,256]{1,0:T(8,128)}, u32[]{:S(2)}) copy-start(f32[512,256]{1,0:T(8,128)} %get-tuple-element.15) | copy-start | bytes 1572868

commit v2 on v1

--- a/solution.py
+++ b/solution.py
@@ -112,7 +112,7 @@
 
 def early_kernel(
     doc, q_hbm, k_hbm, v_hbm, a_hbm, g_hbm, ln_hbm,
-    delta_out, dqt_out, dkv_out,
+    delta_out, dqt_out, dkv_out, need_out,
     q, g, a, k, v, k_t, ln, delta, bias, dq_t, dkv, sem_q, sem_g, sem_a, sem_s, sem_o,
 ):
     small = [
@@ -140,6 +140,10 @@
         copy_a(h).start()
         if h < HEADS_A:
             copy_q(h).start()
+    need = jnp.int32(0)
+    for d in range(2, doc.shape[0] // NB):
+        need = jnp.where(doc[d * NB] == doc[d * NB - NB - 1], 1, need)
+    need_out[0] = need
     fill_bias(doc, bias)
     dkv[...] = jnp.zeros((TOK, 2 * DH), F32)
     for c in small:
@@ -181,9 +185,10 @@
             jax.ShapeDtypeStruct((H, TOK), F32),
             jax.ShapeDtypeStruct((HEADS_A, DH, TOK), F32),
             jax.ShapeDtypeStruct((TOK, 2 * DH), F32),
+            jax.ShapeDtypeStruct((1,), jnp.int32),
         ),
         in_specs=[SMEM] + [ANY] * 6,
-        out_specs=(ANY,) * 3,
+        out_specs=(ANY, ANY, ANY, SMEM),
         scratch_shapes=[
             big, big, big,
             pltpu.VMEM((TOK, DH), BF16),
@@ -205,70 +210,55 @@
     )(doc, q, k, v, a, g, ln_t)
 
 
-def remote_kernel(
-    doc, q, g, ln, delta_hbm, k1, v1, k2, v2,
-    dqt_out, near_out, far_out,
-    delta, k, k_t, ln2, dq_t, acc, near, far, sem_o, sem_s,
+def dead_rows(ln, n_rows, toks):
+    tok_live = lax.broadcasted_iota(jnp.int32, (H, toks), 1) < n_rows * BLK
+    return jnp.where(tok_live, ln[:, 0:toks] * LOG2E, -FAR)
+
+
+def load_keys(k_in, keys, count, k, k_t, acc):
+    key_row = lax.broadcasted_iota(jnp.int32, (keys, DH), 0)
+    live = key_row >= keys - count * BLK
+    k[0:keys, :] = jnp.where(live, k_in[TOK - keys :, :], jnp.zeros((keys, DH), BF16))
+    k_t[:, 0:keys] = jnp.transpose(k[0:keys, :])
+    acc[0:keys, :] = jnp.zeros((keys, 2 * DH), F32)
+    return live
+
+
+def remote_head(h, q, g, v_in, ln2, delta, k, k_t, acc, keys, toks):
+    x, dk, dv = piece(
+        k[0:keys, :], v_in[TOK - keys :, :], k_t[:, 0:keys], q[0:toks, cols(h)], g[0:toks, cols(h)],
+        ln2[row(h), 0:toks], delta[row(h), 0:toks], None,
+    )
+    acc[0:keys, 0:DH] += dk
+    acc[0:keys, DH:] += dv
+    return x
+
+
+def store_keys(out, acc, keys, live):
+    zero = jnp.zeros((keys, DH), F32)
+    here = slice(TOK - keys, TOK)
+    out[here, 0:DH] = jnp.where(live, acc[0:keys, 0:DH] * SCALE, zero).astype(BF16)
+    out[here, DH:] = jnp.where(live, acc[0:keys, DH:], zero).astype(BF16)
+    if keys < TOK:
+        out[0 : TOK - keys, :] = jnp.zeros((TOK - keys, 2 * DH), BF16)
+
+
+def near_kernel(
+    doc, q, g, ln, delta, k_in, v_in,
+    dqt_out, near_out,
+    k, k_t, ln2, dq_t, acc, near, sem,
 ):
-    c_delta = pltpu.make_async_copy(delta_hbm, delta, sem_s.at[0])
-    c_delta.start()
     n_keys, n_rows = crossing(doc, 1)
-    n_far, _ = crossing(doc, 2)
-
-    def copy_o(h, toks):
-        return pltpu.make_async_copy(dq_t.at[h, :, pl.ds(0, toks)], dqt_out.at[h, :, pl.ds(0, toks)], sem_o.at[h])
-
-    def mask_rows(toks):
-        tok_live = lax.broadcasted_iota(jnp.int32, (H, toks), 1) < n_rows * BLK
-        ln2[:, 0:toks] = jnp.where(tok_live, ln[:, 0:toks] * LOG2E, -FAR)
-
-    def load_keys(k_in, v_in, keys, count):
-        here = slice(TOK - keys, TOK)
-        key_row = lax.broadcasted_iota(jnp.int32, (keys, DH), 0)
-        live = key_row >= keys - count * BLK
-        k[0:keys, :] = jnp.where(live, k_in[here, :], jnp.zeros((keys, DH), BF16))
-        k_t[:, 0:keys] = jnp.transpose(k[0:keys, :])
-        acc[0:keys, :] = jnp.zeros((keys, 2 * DH), F32)
-        return here, live
-
-    def head(h, v, keys, toks):
-        x, dk, dv = piece(
-            k[0:keys, :], v, k_t[:, 0:keys], q[0:toks, cols(h)], g[0:toks, cols(h)],
-            ln2[row(h), 0:toks], delta[row(h), 0:toks], None,
-        )
-        acc[0:keys, 0:DH] += dk
-        acc[0:keys, DH:] += dv
-        return x
-
-    def store_keys(out, keys, total, live):
-        zero = jnp.zeros((keys, DH), F32)
-        here = slice(total - keys, total)
-        out[here, 0:DH] = jnp.where(live, acc[0:keys, 0:DH] * SCALE, zero).astype(BF16)
-        out[here, DH:] = jnp.where(live, acc[0:keys, DH:], zero).astype(BF16)
-        if keys < total:
-            out[0 : total - keys, :] = jnp.zeros((total - keys, 2 * DH), BF16)
 
     def run(keys, toks):
-        here, live = load_keys(k1, v1, keys, n_keys)
-        mask_rows(toks)
+        live = load_keys(k_in, keys, n_keys, k, k_t, acc)
+        ln2[:, 0:toks] = dead_rows(ln, n_rows, toks)
 
         @pl.loop(0, H, unroll=2)
         def _(h):
-            dq_t[h, :, 0:toks] = head(h, v1[here, :], keys, toks)
-
-        store_keys(near, keys, TOK, live)
-
-    def run_far():
-        here, live = load_keys(k2, v2, FAR_TOK, n_far)
-        mask_rows(TOK)
-
-        @pl.loop(0, H)
-        def _(h):
-            x = head(h, v2[here, :], FAR_TOK, TOK)
-            tok_live = lax.broadcasted_iota(jnp.int32, (DH, TOK), 1) < n_rows * BLK
-            dq_t[h] = jnp.where(tok_live, dq_t[h] + x, 0.0)
-
-        store_keys(far, FAR_TOK, FAR_TOK, live)
+            dq_t[h, :, 0:toks] = remote_head(h, q, g, v_in, ln2, delta, k, k_t, acc, keys, toks)
+
+        store_keys(near, acc, keys, live)
 
     few_keys = n_keys * BLK <= HALF
     few_rows = n_rows * BLK <= HALF
@@ -277,59 +267,90 @@
     def _():
         near[...] = jnp.zeros((TOK, 2 * DH), BF16)
 
-    @pl.when(n_far == 0)
-    def _():
-        far[...] = jnp.zeros((FAR_TOK, 2 * DH), BF16)
-
-    c_delta.wait()
     for keys in (HALF, TOK):
         for toks in (HALF, TOK):
             ok = (n_keys > 0) & (few_keys == (keys == HALF)) & (few_rows == (toks == HALF))
             pl.when(ok)(functools.partial(run, keys, toks))
-    pl.when(n_far > 0)(run_far)
-    tail = [
-        pltpu.make_async_copy(near, near_out, sem_s.at[0]),
-        pltpu.make_async_copy(far, far_out, sem_s.at[1]),
-    ]
-    for c in tail:
-        c.start()
-    c_dq = pltpu.make_async_copy(dq_t, dqt_out, sem_o.at[0])
+    c_near = pltpu.make_async_copy(near, near_out, sem.at[0])
+    c_dq = pltpu.make_async_copy(dq_t, dqt_out, sem.at[1])
+    c_near.start()
 
     @pl.when(n_keys > 0)
     def _():
         c_dq.start()
         c_dq.wait()
 
-    for c in tail:
-        c.wait()
-
-
-def remote_pieces(doc, q, g, ln_t, delta, k1, v1, k2, v2):
+    c_near.wait()
+
+
+def remote_scratch():
+    return [
+        pltpu.VMEM((TOK, DH), BF16),
+        pltpu.VMEM((DH, TOK), BF16),
+        pltpu.VMEM((H, TOK), F32),
+        pltpu.VMEM((H, DH, TOK), F32),
+        pltpu.VMEM((TOK, 2 * DH), F32),
+        pltpu.VMEM((TOK, 2 * DH), BF16),
+        pltpu.SemaphoreType.DMA((2,)),
+    ]
+
+
+def near_pieces(doc, q, g, ln_t, delta, k1, v1):
     return pl.pallas_call(
-        remote_kernel,
-        name="remote",
+        near_kernel,
+        name="near",
         out_shape=(
             jax.ShapeDtypeStruct((H, DH, TOK), F32),
             jax.ShapeDtypeStruct((TOK, 2 * DH), BF16),
-            jax.ShapeDtypeStruct((FAR_TOK, 2 * DH), BF16),
         ),
-        in_specs=[SMEM] + [VMEM] * 3 + [ANY] + [VMEM] * 4,
-        out_specs=(ANY, ANY, ANY),
-        scratch_shapes=[
-            pltpu.VMEM((H, TOK), F32),
-            pltpu.VMEM((TOK, DH), BF16),
-            pltpu.VMEM((DH, TOK), BF16),
-            pltpu.VMEM((H, TOK), F32),
-            pltpu.VMEM((H, DH, TOK), F32),
-            pltpu.VMEM((TOK, 2 * DH), F32),
-            pltpu.VMEM((TOK, 2 * DH), BF16),
-            pltpu.VMEM((FAR_TOK, 2 * DH), BF16),
-            pltpu.SemaphoreType.DMA((1,)),
-            pltpu.SemaphoreType.DMA((2,)),
-        ],
+        in_specs=[SMEM] + [VMEM] * 6,
+        out_specs=(ANY, ANY),
+        scratch_shapes=remote_scratch(),
         compiler_params=pltpu.CompilerParams(vmem_limit_bytes=VMEM_LIMIT),
         cost_estimate=pl.CostEstimate(flops=4_000_000_000, bytes_accessed=6_000_000, transcendentals=2_000_000),
-    )(doc, q, g, ln_t, delta, k1, v1, k2, v2)
+    )(doc, q, g, ln_t, delta, k1, v1)
+
+
+def far_kernel(
+    doc, q, g, ln, delta, k_in, v_in,
+    dq_out, far_out,
+    k, k_t, ln2, dq_t, acc, far, sem,
+):
+    n_keys, n_rows = crossing(doc, 2)
+    dq_out[...] = jnp.zeros((TOK, H * DH), F32)
+    far[...] = jnp.zeros((TOK, 2 * DH), BF16)
+
+    @pl.when(n_keys > 0)
+    def _():
+        live = load_keys(k_in, TOK, n_keys, k, k_t, acc)
+        ln2[...] = dead_rows(ln, n_rows, TOK)
+
+        @pl.loop(0, H)
+        def _(h):
+            x = remote_head(h, q, g, v_in, ln2, delta, k, k_t, acc, TOK, TOK)
+            dq_out[:, cols(h)] = jnp.transpose(x) * SCALE
+
+        store_keys(far, acc, TOK, live)
+
+    c = pltpu.make_async_copy(far, far_out, sem.at[0])
+    c.start()
+    c.wait()
+
+
+def far_pieces(doc, q, g, ln_t, delta, k2, v2):
+    return pl.pallas_call(
+        far_kernel,
+        name="far",
+        out_shape=(
+            jax.ShapeDtypeStruct((TOK, H * DH), F32),
+            jax.ShapeDtypeStruct((TOK, 2 * DH), BF16),
+        ),
+        in_specs=[SMEM] + [VMEM] * 6,
+        out_specs=(VMEM, ANY),
+        scratch_shapes=remote_scratch(),
+        compiler_params=pltpu.CompilerParams(vmem_limit_bytes=VMEM_LIMIT),
+        cost_estimate=pl.CostEstimate(flops=4_000_000_000, bytes_accessed=6_000_000, transcendentals=2_000_000),
+    )(doc, q, g, ln_t, delta, k2, v2)
 
 
 def late_kernel(
@@ -398,19 +419,24 @@
     ln_t = log_norm.T
     near_k = moved(key_input, 1)
     near_v = moved(value_input, 1)
-    far_k = moved(key_input, 2)
-    far_v = moved(value_input, 2)
-    delta, dqt, dkv_a = early(doc_block, queries, key_input, value_input, attn_out, out_grad, ln_t)
-    rem, part1, part2 = remote_pieces(doc_block, queries, out_grad, ln_t, delta, near_k, near_v, far_k, far_v)
-    back1 = moved(part1, -1)
-    back2 = moved(part2, -2)
+    delta, dqt, dkv_a, need = early(doc_block, queries, key_input, value_input, attn_out, out_grad, ln_t)
+    rem, part = near_pieces(doc_block, queries, out_grad, ln_t, delta, near_k, near_v)
+    back = moved(part, -1)
     dq, dkv_b = late(doc_block, queries, key_input, value_input, out_grad, ln_t, delta, dqt, rem)
     dkv = dkv_a + dkv_b
-    dk = dkv[:, :DH] * SCALE + back1[:, :DH].astype(F32)
-    dv = dkv[:, DH:] + back1[:, DH:].astype(F32)
-    dk = jnp.concatenate([dk[:BLK], dk[BLK:] + back2[:, :DH].astype(F32)], axis=0)
-    dv = jnp.concatenate([dv[:BLK], dv[BLK:] + back2[:, DH:].astype(F32)], axis=0)
-    return dq, dk.astype(BF16), dv.astype(BF16)
+    dk = dkv[:, :DH] * SCALE + back[:, :DH].astype(F32)
+    dv = dkv[:, DH:] + back[:, DH:].astype(F32)
+
+    def far_step(_, grads):
+        keys, values, grads = lax.optimization_barrier((key_input, value_input, grads))
+        far_k = moved(keys, 2)
+        far_v = moved(values, 2)
+        dq_far, far_part = far_pieces(doc_block, queries, out_grad, ln_t, delta, far_k, far_v)
+        far_back = moved(far_part, -2).astype(F32)
+        adds = (dq_far, far_back[:, :DH], far_back[:, DH:])
+        return tuple((x.astype(F32) + y).astype(BF16) for x, y in zip(grads, adds))
+
+    return lax.fori_loop(0, need[0], far_step, (dq, dk.astype(BF16), dv.astype(BF16)))
 
 
 def solution(mesh):

time: 35.3 us -> 28.5 us (0.81)
  the two profiles are of different devices: /device:TPU:1 before, /device:TPU:2 now
where the time goes in v2:
time: 28.5 us; the launch traced here: 28 us
  Pallas kernels  14.3 us (50%)
  starting transfers between devices  9.41 us (33%)
  waiting for transfers between devices  1.49 us (5%)
  local copies, waits for them, and re-layouts  1.07 us (4%)
  loops' own time  0.82 us (3%)
  between operations  0.81 us (3%)
    ppermute x3, starting transfers between devices, moved(): lax.ppermute(value, 'seq', [(i, (i + by) % count) for i in range(count)])  9.41 us
    pallas_call x1, Pallas kernels, early(): pl.pallas_call(early_kernel, name='early', out_shape=(jax.ShapeDtypeStruc...  8.81 us
    pallas_call x1, Pallas kernels, late(): pl.pallas_call(late_kernel, name='late', out_shape=(jax.ShapeDtypeStruct(...  4.78 us
    ppermute x3, waiting for transfers between devices, moved(): lax.ppermute(value, 'seq', [(i, (i + by) % count) for i in range(count)])  1.49 us
    unnamed x26, local copies, waits for them, and re-layouts  1.07 us
    another operation x1, loops' own time, local(): lax.fori_loop(0, need[0], far_step, (dq, dk.astype(BF16), dv.astype(BF16)))  0.82 us
    pallas_call x1, Pallas kernels, near_pieces(): pl.pallas_call(near_kernel, name='near', out_shape=(jax.ShapeDtypeStruct(...  0.66 us
  transfers between devices with their start and end apart: 3, of which 2 were waited for; matrix products, arithmetic and copies ran while one was open for 0% of the time, Pallas kernels for 49%

profile of v2, /device:TPU:2, one launch (start us, length us, event | category | flops | bytes accessed | tf_op | source)
XLA Modules:
  0.0 28.0 jit_solution(3065179379379164944)
XLA Ops:
  0.6 0.1 collective-permute-start.3
  0.7 1.7 %collective-permute-start.4 = (bf16[512,128]{1,0:T(8,128)(2,1)}, bf16[512,128]{1,0:T(8,128)(2,1)S(1)}, u32[]{:S(2)}, u32[]{:S(2)}) collective-permute-start(bf16[512,128]{1,0:T(8,128)(2,1)} %v.1), channel_id=1, source_target_pairs={{0,4},{4,8},{8,12},{12,16},{16,20},{20,24},{24,28},{28,32},{32,36}... | collective-permute-start | bytes 393224 | tf_op jit(solution)/shard_map/ppermute | solution.py:415
  2.4 0.0 copy-start.5
  2.4 0.0 copy-start.6
  2.4 0.0 copy-start.10
  2.4 0.0 copy-start.11
  2.4 8.8 %early.1 = (f32[8,512]{1,0:T(8,128)S(1)}, f32[4,128,512]{2,1,0:T(8,128)}, f32[512,256]{1,0:T(8,128)}, s32[1]{0:T(128)}) custom-call(s32[256]{0:T(256)} %doc.5, bf16[512,1024]{1,0:T(8,128)(2,1)} %q.3, bf16[512,128]{1,0:T(8,128)(2,1)} %k.1, bf16[512,128]{1,0:T(8,128)(2,1)} %v.1, bf16[512,1024]{1,0:T(8,128)(2,1)} %a_hbm.1, bf16[512,1024]{1,0:T(8,128)(2,1)} %g.3, ...), custom_call_target="tpu_custom_call" | custom-call | flops 4000000000 | bytes 6000000 | tf_op jit(solution)/shard_map/early/pallas_call | solution.py:181
  11.2 0.0 copy-start.13
  11.2 0.1 collective-permute-done.3.k_in
  11.3 1.4 %collective-permute-done.4.v_in = bf16[512,128]{1,0:T(8,128)(2,1)S(1)} collective-permute-done((bf16[512,128]{1,0:T(8,128)(2,1)}, bf16[512,128]{1,0:T(8,128)(2,1)S(1)}, u32[]{:S(2)}, u32[]{:S(2)}) %collective-permute-start.4) | collective-permute-done | bytes 131104 | tf_op jit(solution)/shard_map/ppermute | solution.py:415
  12.7 0.0 copy-done.5
  12.7 0.0 copy-done.6
  12.7 0.0 copy-done.10
  12.7 0.0 copy-done.11
  12.7 0.0 copy-start
  12.8 0.0 copy-start.8
  12.8 0.0 copy-start.9
  12.8 0.0 copy-start.12
  12.8 0.7 %near.1 = (f32[8,128,512]{2,1,0:T(8,128)S(1)}, bf16[512,256]{1,0:T(8,128)(2,1)S(1)}) custom-call(s32[256]{0:T(256)S(1)} %copy-done.11, bf16[512,1024]{1,0:T(8,128)(2,1)S(1)} %copy-done.5, bf16[512,1024]{1,0:T(8,128)(2,1)S(1)} %copy-done.6, f32[8,512]{1,0:T(8,128)S(1)} %bitcast.3, f32[8,512]{1,0:T(8,128)S(1)} %get-tuple-element.225.delta, ...), custom_call_target="tpu_custom_call" | custom-call | flops 4000000000 | bytes 6000000 | tf_op jit(solution)/shard_map/near/pallas_call | solution.py:299
  13.5 0.0 copy-done.13
  13.5 7.6 %collective-permute-start.5 = (bf16[512,256]{1,0:T(8,128)(2,1)S(1)}, bf16[512,256]{1,0:T(8,128)(2,1)S(1)}, u32[]{:S(2)}, u32[]{:S(2)}) collective-permute-start(bf16[512,256]{1,0:T(8,128)(2,1)S(1)} %get-tuple-element.89), channel_id=1, source_target_pairs={{0,252},{4,0},{8,4},{12,8},{16,12},{20,16},{24,20},{28,24},{32,28}... | collective-permute-start | bytes 786440 | tf_op jit(solution)/shard_map/ppermute | solution.py:415
  21.1 0.0 copy-done
  21.1 0.0 copy-done.8
  21.1 0.0 copy-done.9
  21.1 0.0 copy-done.12
  21.1 0.0 copy-start.4
  21.1 4.8 %late.1 = (bf16[512,1024]{1,0:T(8,128)(2,1)S(1)}, f32[512,256]{1,0:T(8,128)S(1)}) custom-call(s32[256]{0:T(256)S(1)} %copy-done.12, bf16[512,1024]{1,0:T(8,128)(2,1)S(1)} %copy-done.5, bf16[512,128]{1,0:T(8,128)(2,1)S(1)} %copy-done.8, bf16[512,128]{1,0:T(8,128)(2,1)S(1)} %copy-done.9, bf16[512,1024]{1,0:T(8,128)(2,1)S(1)} %copy-done.6, ...), custom_call_target="tpu_custom_call" | custom-call | flops 4000000000 | bytes 5000000 | tf_op jit(solution)/shard_map/late/pallas_call | solution.py:391
  25.9 0.0 copy-done.4
  25.9 0.1 add.21
  26.0 0.0 collective-permute-done.5
  26.0 0.1 fusion.2
  26.1 0.8 %while.14 = (s32[]{:T(128)}, bf16[512,1024]{1,0:T(8,128)(2,1)S(1)}, bf16[512,128]{1,0:T(8,128)(2,1)S(1)}, bf16[512,128]{1,0:T(8,128)(2,1)S(1)}, s32[]{:T(128)}, ...) while((s32[]{:T(128)}, bf16[512,1024]{1,0:T(8,128)(2,1)S(1)}, ...), condition=%wide.region_1.0_spmd, body=%wide.region_0.0_spmd.sunk | while | flops 4002097152 | bytes 18321048 | solution.py:439
  26.9 0.0 copy-start.1
  26.9 0.0 copy-start.2
  27.0 0.0 copy-start.3
  27.0 0.9 %copy-done.1 = bf16[512,1024]{1,0:T(8,128)(2,1)} copy-done((bf16[512,1024]{1,0:T(8,128)(2,1)}, bf16[512,1024]{1,0:T(8,128)(2,1)S(1)}, u32[]{:S(2)}) %copy-start.1) | copy-done | bytes 1048600
  27.9 0.0 copy-done.2
  27.9 0.0 copy-done.3
Async XLA Ops:
  0.6 10.7 %collective-permute-start.3 = (bf16[512,128]{1,0:T(8,128)(2,1)}, bf16[512,128]{1,0:T(8,128)(2,1)S(1)}, u32[]{:S(2)}, u32[]{:S(2)}) collective-permute-start(bf16[512,128]{1,0:T(8,128)(2,1)} %k.1), channel_id=1, source_target_pairs={{0,4},{4,8},{8,12},{12,16},{16,20},{20,24},{24,28},{28,32},{32,36}... | collective-permute-start | bytes 393224 | tf_op jit(solution)/shard_map/ppermute | solution.py:415
  0.7 12.0 %collective-permute-start.4 = (bf16[512,128]{1,0:T(8,128)(2,1)}, bf16[512,128]{1,0:T(8,128)(2,1)S(1)}, u32[]{:S(2)}, u32[]{:S(2)}) collective-permute-start(bf16[512,128]{1,0:T(8,128)(2,1)} %v.1), channel_id=1, source_target_pairs={{0,4},{4,8},{8,12},{12,16},{16,20},{20,24},{24,28},{28,32},{32,36}... | collective-permute-start | bytes 393224 | tf_op jit(solution)/shard_map/ppermute | solution.py:415
  2.4 10.3 %copy-start.5 = (bf16[512,1024]{1,0:T(8,128)(2,1)S(1)}, bf16[512,1024]{1,0:T(8,128)(2,1)}, u32[]{:S(2)}) copy-start(bf16[512,1024]{1,0:T(8,128)(2,1)} %q.3) | copy-start | bytes 3145732
  2.4 10.3 %copy-start.6 = (bf16[512,1024]{1,0:T(8,128)(2,1)S(1)}, bf16[512,1024]{1,0:T(8,128)(2,1)}, u32[]{:S(2)}) copy-start(bf16[512,1024]{1,0:T(8,128)(2,1)} %g.3) | copy-start | bytes 3145732
  2.4 10.3 %copy-start.10 = (f32[512,8]{0,1:T(8,128)S(1)}, f32[512,8]{0,1:T(8,128)}, u32[]{:S(2)}) copy-start(f32[512,8]{0,1:T(8,128)} %param.14) | copy-start | bytes 49156
  2.4 10.3 %copy-start.11 = (s32[256]{0:T(256)S(1)}, s32[256]{0:T(256)}, u32[]{:S(2)}) copy-start(s32[256]{0:T(256)} %doc.5) | copy-start | bytes 3076
  11.2 2.2 %copy-start.13 = (f32[8,512]{1,0:T(8,128)}, f32[8,512]{1,0:T(8,128)S(1)}, u32[]{:S(2)}) copy-start(f32[8,512]{1,0:T(8,128)S(1)} %get-tuple-element.225.delta) | copy-start | bytes 49156
  12.7 8.4 %copy-start = (f32[4,128,512]{2,1,0:T(8,128)S(1)}, f32[4,128,512]{2,1,0:T(8,128)}, u32[]{:S(2)}) copy-start(f32[4,128,512]{2,1,0:T(8,128)} %get-tuple-element.84.own_a) | copy-start | bytes 3145732
  12.8 8.4 %copy-start.8 = (bf16[512,128]{1,0:T(8,128)(2,1)S(1)}, bf16[512,128]{1,0:T(8,128)(2,1)}, u32[]{:S(2)}) copy-start(bf16[512,128]{1,0:T(8,128)(2,1)} %k.1) | copy-start | bytes 393220
  12.8 8.4 %copy-start.9 = (bf16[512,128]{1,0:T(8,128)(2,1)S(1)}, bf16[512,128]{1,0:T(8,128)(2,1)}, u32[]{:S(2)}) copy-start(bf16[512,128]{1,0:T(8,128)(2,1)} %v.1) | copy-start | bytes 393220
  12.8 8.3 %copy-start.12 = (s32[256]{0:T(256)S(1)}, s32[256]{0:T(256)}, u32[]{:S(2)}) copy-start(s32[256]{0:T(256)} %doc.5) | copy-start | bytes 3076
  13.5 12.5 %collective-permute-start.5 = (bf16[512,256]{1,0:T(8,128)(2,1)S(1)}, bf16[512,256]{1,0:T(8,128)(2,1)S(1)}, u32[]{:S(2)}, u32[]{:S(2)}) collective-permute-start(bf16[512,256]{1,0:T(8,128)(2,1)S(1)} %get-tuple-element.89), channel_id=1, source_target_pairs={{0,252},{4,0},{8,4},{12,8},{16,12},{20,16},{24,20},{28,24},{32,28}... | collective-permute-start | bytes 786440 | tf_op jit(solution)/shard_map/ppermute | solution.py:415
  21.1 4.8 %copy-start.4 = (f32[512,256]{1,0:T(8,128)S(1)}, f32[512,256]{1,0:T(8,128)}, u32[]{:S(2)}) copy-start(f32[512,256]{1,0:T(8,128)} %get-tuple-element.87) | copy-start | bytes 1572868
  26.9 1.0 %copy-start.1 = (bf16[512,1024]{1,0:T(8,128)(2,1)}, bf16[512,1024]{1,0:T(8,128)(2,1)S(1)}, u32[]{:S(2)}) copy-start(bf16[512,1024]{1,0:T(8,128)(2,1)S(1)} %get-tuple-element.262) | copy-start | bytes 3145732
  26.9 1.0 %copy-start.2 = (bf16[512,128]{1,0:T(8,128)(2,1)}, bf16[512,128]{1,0:T(8,128)(2,1)S(1)}, u32[]{:S(2)}) copy-start(bf16[512,128]{1,0:T(8,128)(2,1)S(1)} %get-tuple-element.264) | copy-start | bytes 393220
  27.0 1.0 %copy-start.3 = (bf16[512,128]{1,0:T(8,128)(2,1)}, bf16[512,128]{1,0:T(8,128)(2,1)S(1)}, u32[]{:S(2)}) copy-start(bf16[512,128]{1,0:T(8,128)(2,1)S(1)} %get-tuple-element.263) | copy-start | bytes 393220
